TPU v7x, 256 devices: a whole 4x4x8 slice. The times are simulated.
256 devices in a mesh: tm: 32 (over y, z), eval: 8 (over x, core).
Axes of the slice: x: 4, y: 4, z: 8, core: 2. Of those that a mesh axis runs over, the one named last changes fastest.
Arguments:
- hidden: bfloat16 [512, 1024, 1536], P('tm', 'eval'), may hold values from -9 to 9
- modulation: float32 [512, 2, 1536], P('tm'), may hold values from -2 to 3
- head_weight: bfloat16 [64, 1536], replicated, may hold values from -1 to 1
- real_score: bfloat16 [64, 21, 16, 4096], P('eval', None, None, 'tm'), may hold values from -152917 to 152917
- fake_score: bfloat16 [64, 21, 16, 4096], P('eval', None, None, 'tm'), may hold values from -152917 to 152917
- window_start: int32 [64], P('eval'), may hold values from 0 to 491, as said below
- timestep: int32 [64], P('eval'), may hold values from 20 to 999
Outputs:
- d_hidden: bfloat16 [512, 1024, 1536], P('tm', 'eval')
- head_grad: float32 [64, 1536], replicated
- mod_grad: float32 [512, 2, 1536], P('tm')
Inputs may be any that keep to these rules, and one draw needn't show every extreme that they name: `window_start`: every window lies inside the rollout; one window starts at frame 0 and one at the last possible frame.
All inputs are finite; a program needn't handle non-finite values.
Results may differ from a plain program's by a relative error of at most 0.0012.
The roundings to bfloat16 on the way count: a program that leaves them out, or rounds other values in their place, can miss the bound.
Values may be sent and summed in bfloat16 or wider, within the bound.
No kernel may reach another device: no remote copies, remote signals or barrier semaphores. Data moves between devices by JAX's collectives and lax.ppermute only.
A program may use at most 128 MiB of HBM per device.

v0:
```python
import jax
import jax.numpy as jnp
from jax import lax
from jax.sharding import PartitionSpec as P

C = 16
PATCH = 4
WIN = 21
TOK = 1024


def layer_norm(values_in):
    values = values_in.astype(jnp.float32)
    center = jnp.mean(values, axis=-1, keepdims=True)
    shifted = values - center
    inv_std = lax.rsqrt(jnp.mean(shifted * shifted, axis=-1, keepdims=True) + 1e-06)
    return (shifted * inv_std, inv_std)


def per_device(hidden, modulation, head_weight, real_score, fake_score, window_start, timestep):
    frames_dev, tok_dev, width = hidden.shape
    shift = modulation[:, 0][:, None, :]
    scale = modulation[:, 1][:, None, :]
    normed, inv_std = layer_norm(hidden)
    adapted = (normed * (1.0 + scale) + shift).astype(jnp.bfloat16)
    head_out = jnp.einsum("ftd,od->fto", adapted, head_weight, preferred_element_type=jnp.float32)
    latent = head_out.astype(jnp.bfloat16).reshape(frames_dev, tok_dev, C, PATCH)
    latent = latent.transpose(0, 2, 1, 3).reshape(frames_dev, C, tok_dev * PATCH)
    frame_whole = lax.all_gather(latent, "eval", axis=2, tiled=True)
    latent_all = lax.all_to_all(frame_whole, "tm", split_axis=2, concat_axis=0, tiled=True)
    pixel_block = latent_all.shape[2]
    frame_index = window_start[:, None] + jnp.arange(WIN, dtype=jnp.int32)[None, :]
    window_latent = latent_all[frame_index].astype(jnp.float32)
    real_values = real_score.astype(jnp.float32)
    fake_values = fake_score.astype(jnp.float32)
    abs_sums = jnp.sum(jnp.abs(window_latent - real_values), axis=(1, 2, 3))
    totals = lax.psum(abs_sums, "tm")
    normalizer = totals / (WIN * C * PATCH * TOK) + 1e-05
    weight = timestep.astype(jnp.float32) / 1000.0 / normalizer
    window_grad = weight[:, None, None, None] * (fake_values - real_values)
    group_grad = (
        jnp.zeros(latent_all.shape, jnp.float32)
        .at[frame_index.reshape(-1)]
        .add(window_grad.reshape(-1, C, pixel_block))
    )
    home = lax.all_to_all(group_grad, "tm", split_axis=0, concat_axis=2, tiled=True)
    owner_grad = lax.psum_scatter(home, "eval", scatter_dimension=2, tiled=True)
    upstream = owner_grad.reshape(frames_dev, C, tok_dev, PATCH).transpose(0, 2, 1, 3)
    upstream = upstream.reshape(frames_dev, tok_dev, C * PATCH).astype(jnp.bfloat16)
    d_adapted = jnp.einsum("fto,od->ftd", upstream, head_weight, preferred_element_type=jnp.float32)
    head_part = jnp.einsum("fto,ftd->od", upstream, adapted, preferred_element_type=jnp.float32)
    mod_part = jnp.stack([jnp.sum(d_adapted, axis=1), jnp.sum(d_adapted * normed, axis=1)], axis=1)
    head_grad = lax.psum(head_part, ("tm", "eval"))
    mod_grad = lax.psum(mod_part, "eval")
    d_normed = d_adapted * (1.0 + scale)
    d_hidden = inv_std * (
        d_normed
        - jnp.mean(d_normed, axis=-1, keepdims=True)
        - normed * jnp.mean(d_normed * normed, axis=-1, keepdims=True)
    )
    return (d_hidden.astype(jnp.bfloat16), head_grad, mod_grad)


def solution(mesh):
    placed = (
        P("tm", "eval", None),
        P("tm", None, None),
        P(),
        P("eval", None, None, "tm"),
        P("eval", None, None, "tm"),
        P("eval"),
        P("eval"),
    )
    return jax.shard_map(
        per_device,
        mesh=mesh,
        in_specs=placed,
        out_specs=(P("tm", "eval", None), P(), P("tm", None, None)),
        check_vma=False,
    )
```

profile of v0, /device:TPU:1, one launch (start us, length us, event | category | flops | bytes accessed | tf_op | source)
XLA Modules:
  0.0 757.5 jit_solution(7772980234880290092)
XLA Ops:
  7.2 0.0 copy-start
  7.2 0.0 all-gather.2.cloned.1.call-start
  7.2 0.0 copy-start.1
  7.2 3.8 convert_reduce_fusion
  11.1 4.6 fusion.13
  15.7 0.2 fusion.33
  15.9 3.1 fusion.24
  19.0 3.2 copy.49
  22.2 2.3 copy.50
  24.5 0.0 all-gather.2.cloned.1.call-update
  24.5 32.2 %all-gather.2.cloned.1.call-done = bf16[16,16,4096]{2,1,0:T(8,128)(2,1)} async-done(((bf16[16,16,512]{2,1,0:T(8,128)(2,1)}), bf16[16,16,4096]{2,1,0:T(8,128)(2,1)}) %all-gather.2.cloned.1.call-update) | async-done | bytes 2097168 | tf_op jit(solution)/shard_map/all_gather | solution.py:29
  56.7 15.4 %copy.51 = bf16[16,16,4096]{1,0,2:T(8,128)(2,1)} copy(bf16[16,16,4096]{2,1,0:T(8,128)(2,1)} %all-gather.2.cloned.1.call-done) | data formatting | bytes 4194304 | tf_op jit(solution)/shard_map/all_gather | solution.py:29
  72.0 20.8 %reshape.132 = bf16[32,2,16384]{2,1,0:T(2,128)(2,1)} reshape(bf16[4096,16,16]{2,1,0:T(8,128)(2,1)} %bitcast.43) | data formatting | bytes 4194304
  92.8 9.6 %all-to-all-start = ((bf16[32,2,16384]{2,1,0:T(2,128)(2,1)}), bf16[32,2,16384]{2,1,0:T(2,128)(2,1)S(1)}, u32[]{:S(2)}, u32[]{:S(2)}) async-start(bf16[32,2,16384]{2,1,0:T(2,128)(2,1)} %reshape.132), calls=%async_computation | async-start | bytes 4194304 | tf_op jit(solution)/shard_map/all_to_all | solution.py:30
  102.4 0.0 reduce-scatter.2.cloned.1.call-start
  102.5 0.1 compare_select_fusion
  102.5 0.1 reshape.114
  102.6 0.1 iota_add_fusion
  102.7 0.1 add.106
  102.8 48.5 %all-to-all-done = bf16[32,2,16384]{2,1,0:T(2,128)(2,1)S(1)} async-done(((bf16[32,2,16384]{2,1,0:T(2,128)(2,1)}), bf16[32,2,16384]{2,1,0:T(2,128)(2,1)S(1)}, u32[]{:S(2)}, u32[]{:S(2)}) %all-to-all-start) | async-done | bytes 2097184 | tf_op jit(solution)/shard_map/all_to_all | solution.py:30
  151.3 14.4 %reshape.133 = bf16[4096,16,16]{2,1,0:T(8,128)(2,1)} reshape(bf16[32,2,16384]{2,1,0:T(2,128)(2,1)S(1)} %all-to-all-done) | data formatting | bytes 4194304
  165.7 14.4 %copy.53 = bf16[32,16,16,128]{3,2,1,0:T(8,128)(2,1)S(1)} copy(bf16[32,16,16,128]{2,1,3,0:T(8,128)(2,1)} %bitcast.44) | data formatting | bytes 4194304 | tf_op jit(solution)/shard_map/all_to_all | solution.py:30
  180.1 1.6 gather_fusion
  181.7 1.4 fusion.22
  183.1 60.2 %psum.21 = f32[8]{0:T(128)S(1)} all-reduce(f32[8]{0:T(128)S(1)} %fusion.22), channel_id=1, replica_groups=mesh['tm'=32,'eval'=8] {'tm'}, use_global_device_ids=true, to_apply=%region_3.0 | all-reduce | flops 8 | bytes 64 | tf_op jit(solution)/shard_map/psum | solution.py:37
  243.4 1.3 fusion.23
  244.7 2.3 broadcast_in_dim.2
  247.0 19.7 %scatter_fusion = f32[512,16,128]{2,1,0:T(8,128)} fusion(f32[512,16,128]{2,1,0:T(8,128)} %broadcast_in_dim.2, s32[168]{0:T(256)S(1)} %bitcast.59, f32[168,16,128]{2,1,0:T(8,128)S(1)} %bitcast.51), kind=kCustom, calls=%fused_computation.1 | custom fusion | flops 344064 | bytes 4129440 | tf_op jit(solution)/shard_map/scatter-add | solution.py:44
  266.7 83.4 %all_to_all.36 = f32[512,16,128]{2,1,0:T(8,128)S(1)} all-to-all(f32[512,16,128]{2,1,0:T(8,128)} %scatter_fusion), channel_id=1, replica_groups=mesh['tm'=32,'eval'=8] {'tm'}, dimensions={0} | all-to-all | bytes 8388608 | tf_op jit(solution)/shard_map/all_to_all | solution.py:46
  350.1 2.5 copy.76
  352.7 0.0 reduce-scatter.2.cloned.1.call-update
  352.7 0.0 all-reduce.5.cloned.1.call-start
  352.7 50.7 %reduce-scatter.2.cloned.1.call-done = f32[16,16,512]{2,1,0:T(8,128)} async-done(((f32[16,16,4096]{2,1,0:T(8,128)}), f32[16,16,512]{2,1,0:T(8,128)}) %reduce-scatter.2.cloned.1.call-update) | async-done | bytes 524304 | tf_op jit(solution)/shard_map/reduce_scatter | solution.py:47
  403.4 1.1 convert_element_type.43
  404.5 2.8 copy.55
  407.3 4.0 copy.56
  411.3 0.0 slice-start.1
  411.3 10.1 %fusion.12 = (f32[16,1536]{1,0:T(8,128)S(1)}, f32[16,128]{1,0:T(8,128)S(1)}, f32[16,128]{1,0:T(8,128)S(1)}, f32[16,1536]{1,0:T(8,128)S(1)}, f32[16,128,1536]{2,1,0:T(8,128)}) fusion(bf16[16,128,1536]{2,1,0:T(8,128)(2,1)} %param.7, f32[16,128]{1,0:T(8,128)S(1)} %add_rsqrt_fusion, f32[16,128]{1,0:T(8,128)S(1)} %broadcast_multiply_fusion.2, ...), kind=kOutput, calls=%fused_computation.16 | convolution fusion | flops 434057216 | bytes 19660800 | tf_op jit(solution)/shard_map/fto,od->ftd/dot_general | solution.py:50
  421.4 3.5 fusion.18
  424.9 0.7 pad_maximum_fusion
  425.6 0.0 all-reduce.5.cloned.1.call-update
  425.6 0.0 all-reduce.3.cloned.1.call-start
  425.7 0.5 all-reduce.3.cloned.1.call-update
  426.2 10.5 %fusion.11 = bf16[16,128,1536]{2,1,0:T(8,128)(2,1)} fusion(bf16[16,128,1536]{2,1,0:T(8,128)(2,1)} %param.7, f32[16,128,1536]{2,1,0:T(8,128)} %get-tuple-element.24, f32[16,128]{1,0:T(8,128)S(1)} %broadcast_multiply_fusion, f32[16,128]{1,0:T(8,128)S(1)} %broadcast_multiply_fusion.1, f32[16,1536]{1,0:T(8,128)S(1)} %get-tuple-element.26, ...), kind=kLoop, calls=%fused_computation.15 | loop fusion | flops 28311552 | bytes 25296896 | tf_op jit(solution)/shard_map/convert_element_type | solution.py:61
  436.7 53.9 %all-reduce.5.cloned.1.call-done = f32[16,2,1536]{2,0,1:T(8,128)} async-done(((f32[16,2,1536]{2,0,1:T(8,128)}), f32[16,2,1536]{2,0,1:T(8,128)}) %all-reduce.5.cloned.1.call-update) | async-done | bytes 196624 | tf_op jit(solution)/shard_map/psum | solution.py:54
  490.5 1.8 copy.59
  492.3 256.9 %all-reduce.3.cloned.1.call-done = f32[64,1536]{1,0:T(8,128)} async-done(((f32[64,1536]{1,0:T(8,128)}), f32[64,1536]{1,0:T(8,128)}) %all-reduce.3.cloned.1.call-update) | async-done | bytes 393232 | tf_op jit(solution)/shard_map/psum | solution.py:53
  749.2 1.8 copy.80
  (22 shorter events, 0.1 us)
Async XLA Ops:
  7.2 8.7 %copy-start = (bf16[64,1536]{1,0:T(8,128)(2,1)S(1)}, bf16[64,1536]{1,0:T(8,128)(2,1)}, u32[]{:S(2)}) copy-start(bf16[64,1536]{1,0:T(8,128)(2,1)} %param.9) | copy-start | bytes 589828
  7.2 8.5 %copy-start.3 = (f32[16,2,1536]{2,1,0:T(2,128)S(1)}, f32[16,2,1536]{2,1,0:T(2,128)}, u32[]{:S(2)}) copy-start(f32[16,2,1536]{2,1,0:T(2,128)} %param.8) | copy-start | bytes 589828
  7.2 49.5 %all-gather.2.cloned.1.call-start = ((), (), s32[]{:S(2)}) async-start(), calls=%async_computation.3 | async-start | bytes 2359296 | tf_op jit(solution)/shard_map/all_gather | solution.py:29
  7.2 8.7 %copy-start.1 = (bf16[16,128,1536]{2,1,0:T(8,128)(2,1)S(1)}, bf16[16,128,1536]{2,1,0:T(8,128)(2,1)}, u32[]{:S(2)}) copy-start(bf16[16,128,1536]{2,1,0:T(8,128)(2,1)} %param.7) | copy-start | bytes 18874372
  72.0 30.4 %copy-start.4 = (s32[8]{0:T(128)S(1)}, s32[8]{0:T(128)}, u32[]{:S(2)}) copy-start(s32[8]{0:T(128)} %param.12) | copy-start | bytes 100
  92.8 58.5 %all-to-all-start = ((bf16[32,2,16384]{2,1,0:T(2,128)(2,1)}), bf16[32,2,16384]{2,1,0:T(2,128)(2,1)S(1)}, u32[]{:S(2)}, u32[]{:S(2)}) async-start(bf16[32,2,16384]{2,1,0:T(2,128)(2,1)} %reshape.132), calls=%async_computation | async-start | bytes 4194304 | tf_op jit(solution)/shard_map/all_to_all | solution.py:30
  102.4 301.0 %reduce-scatter.2.cloned.1.call-start = ((), (), s32[]{:S(2)}) async-start(), calls=%async_computation.4 | async-start | bytes 4718592 | tf_op jit(solution)/shard_map/reduce_scatter | solution.py:47
  165.7 16.0 %copy-start.2 = (bf16[8,21,16,128]{3,2,1,0:T(8,128)(2,1)S(1)}, bf16[8,21,16,128]{3,2,1,0:T(8,128)(2,1)}, u32[]{:S(2)}) copy-start(bf16[8,21,16,128]{3,2,1,0:T(8,128)(2,1)} %param.10) | copy-start | bytes 2064388
  165.7 77.7 %copy-start.5 = (s32[8]{0:T(128)S(1)}, s32[8]{0:T(128)}, u32[]{:S(2)}) copy-start(s32[8]{0:T(128)} %param.13) | copy-start | bytes 100
  352.7 137.9 %all-reduce.5.cloned.1.call-start = ((), (), s32[]{:S(2)}) async-start(), calls=%async_computation.6 | async-start | bytes 393216 | tf_op jit(solution)/shard_map/psum | solution.py:54
  407.3 14.2 %slice-start = ((s8[6291456]{0:T(1024)(128)(4,1)}), s8[2097152]{0:T(1024)(128)(4,1)S(1)}, s32[]{:S(2)}) async-start(s8[6291456]{0:T(1024)(128)(4,1)} %bitcast.45), calls=%async_computation.7 | async-start | bytes 4194304
  411.3 10.1 %slice-start.1 = ((s8[6291456]{0:T(1024)(128)(4,1)}), s8[4194304]{0:T(1024)(128)(4,1)S(1)}, s32[]{:S(2)}) async-start(s8[6291456]{0:T(1024)(128)(4,1)} %bitcast.45), calls=%async_computation.8 | async-start | bytes 8388608
  425.6 323.6 %all-reduce.3.cloned.1.call-start = ((), (), s32[]{:S(2)}) async-start(), calls=%async_computation.5 | async-start | bytes 786432 | tf_op jit(solution)/shard_map/psum | solution.py:53
Sparse Core Ops, SparseCore 0:
  24.6 31.9 all-gather.1
  352.8 50.5 reduce-scatter.1
  425.7 64.7 all-reduce.4
  496.5 252.6 all-reduce.2
where the time goes:
time: 760 us; the launch traced here: 758 us
  waiting for transfers between devices  443 us (58%)
  blocking collectives  144 us (19%)
  local copies, waits for them, and re-layouts  87.5 us (12%)
  other arithmetic  43.3 us (6%)
  matrix products  16.6 us (2%)
  between operations  14 us (2%)
  starting transfers between devices  9.73 us (1%)
    psum x1, waiting for transfers between devices, per_device(): head_grad = lax.psum(head_part, ('tm', 'eval'))  257 us
    all_to_all x1, blocking collectives, per_device(): lax.all_to_all(group_grad, 'tm', split_axis=0, concat_axis=2, tiled=True)  83.4 us
    psum x1, blocking collectives, per_device(): totals = lax.psum(abs_sums, 'tm')  60.2 us
    psum x1, waiting for transfers between devices, per_device(): mod_grad = lax.psum(mod_part, 'eval')  53.9 us
    reduce_scatter x1, waiting for transfers between devices, per_device(): owner_grad = lax.psum_scatter(home, 'eval', scatter_dimension=2, tiled=True)  50.7 us
    all_to_all x1, waiting for transfers between devices, per_device(): lax.all_to_all(frame_whole, 'tm', split_axis=2, concat_axis=0, tiled=True)  48.5 us
    unnamed x20, local copies, waits for them, and re-layouts  38.7 us
    all_gather x1, waiting for transfers between devices, per_device(): frame_whole = lax.all_gather(latent, 'eval', axis=2, tiled=True)  32.2 us
  transfers between devices with their start and end apart: 5, of which 5 were waited for; matrix products, arithmetic and copies ran while one was open for 2% of the time, Pallas kernels for 0%

commit v1 on v0

--- a/solution.py
+++ b/solution.py
@@ -51,7 +51,7 @@
     head_part = jnp.einsum("fto,ftd->od", upstream, adapted, preferred_element_type=jnp.float32)
     mod_part = jnp.stack([jnp.sum(d_adapted, axis=1), jnp.sum(d_adapted * normed, axis=1)], axis=1)
     head_grad = lax.psum(head_part, ("tm", "eval"))
-    mod_grad = lax.psum(mod_part, "eval")
+    mod_grad = jnp.sum(lax.all_gather(mod_part, "eval"), axis=0)
     d_normed = d_adapted * (1.0 + scale)
     d_hidden = inv_std * (
         d_normed

time: 760 us -> 716 us (0.942)
  waiting for transfers between devices: 443 us -> 399 us
    psum x1 -> x0, waiting for transfers between devices: 53.9 us -> none  [per_device(): mod_grad = lax.psum(mod_part, 'eval')]
    all_gather x0 -> x1, waiting for transfers between devices: none -> 12.9 us  [per_device(): mod_grad = jnp.sum(lax.all_gather(mod_part, 'eval'), axis=0)]
    unnamed x20 -> x16, local copies, waits for them, and re-layouts: 38.7 us -> 37.8 us
  transfers between devices with their start and end apart: 5 -> 5, of which waited for: 5 -> 5; matrix products, arithmetic and copies ran while one was open for 2% -> 3% of each run, Pallas kernels for 0% -> 0%
where the time goes in v1:
time: 716 us; the launch traced here: 714 us
  waiting for transfers between devices  399 us (56%)
  blocking collectives  144 us (20%)
  local copies, waits for them, and re-layouts  84.1 us (12%)
  other arithmetic  44.9 us (6%)
  matrix products  18.6 us (3%)
  between operations  14 us (2%)
  starting transfers between devices  9.73 us (1%)
    psum x1, waiting for transfers between devices, per_device(): head_grad = lax.psum(head_part, ('tm', 'eval'))  255 us
    all_to_all x1, blocking collectives, per_device(): lax.all_to_all(group_grad, 'tm', split_axis=0, concat_axis=2, tiled=True)  83.4 us
    psum x1, blocking collectives, per_device(): totals = lax.psum(abs_sums, 'tm')  60.2 us
    reduce_scatter x1, waiting for transfers between devices, per_device(): owner_grad = lax.psum_scatter(home, 'eval', scatter_dimension=2, tiled=True)  50.7 us
    all_to_all x1, waiting for transfers between devices, per_device(): lax.all_to_all(frame_whole, 'tm', split_axis=2, concat_axis=0, tiled=True)  48.5 us
    unnamed x16, local copies, waits for them, and re-layouts  37.8 us
    all_gather x1, waiting for transfers between devices, per_device(): frame_whole = lax.all_gather(latent, 'eval', axis=2, tiled=True)  32.2 us
    scatter-add x1, other arithmetic, per_device(): group_grad = jnp.zeros(latent_all.shape, jnp.float32).at[frame_index.resh...  19.7 us
  transfers between devices with their start and end apart: 5, of which 5 were waited for; matrix products, arithmetic and copies ran while one was open for 3% of the time, Pallas kernels for 0%

profile of v1, /device:TPU:1, one launch (start us, length us, event | category | flops | bytes accessed | tf_op | source)
XLA Modules:
  0.0 714.2 jit_solution(7383057094747505891)
XLA Ops:
  7.2 0.0 copy-start
  7.2 0.0 all-gather.4.cloned.1.call-start
  7.2 0.0 copy-start.1
  7.2 3.8 convert_reduce_fusion
  11.1 4.6 fusion.13
  15.7 0.2 fusion.33
  15.9 3.1 fusion.24
  19.0 3.2 copy.57
  22.2 2.3 copy.58
  24.5 0.0 all-gather.4.cloned.1.call-update
  24.5 32.2 %all-gather.4.cloned.1.call-done = bf16[16,16,4096]{2,1,0:T(8,128)(2,1)} async-done(((bf16[16,16,512]{2,1,0:T(8,128)(2,1)}), bf16[16,16,4096]{2,1,0:T(8,128)(2,1)}) %all-gather.4.cloned.1.call-update) | async-done | bytes 2097168 | tf_op jit(solution)/shard_map/all_gather | solution.py:29
  56.7 15.4 %copy.59 = bf16[16,16,4096]{1,0,2:T(8,128)(2,1)} copy(bf16[16,16,4096]{2,1,0:T(8,128)(2,1)} %all-gather.4.cloned.1.call-done) | data formatting | bytes 4194304 | tf_op jit(solution)/shard_map/all_gather | solution.py:29
  72.0 20.8 %reshape.133 = bf16[32,2,16384]{2,1,0:T(2,128)(2,1)} reshape(bf16[4096,16,16]{2,1,0:T(8,128)(2,1)} %bitcast.44) | data formatting | bytes 4194304
  92.8 9.6 %all-to-all-start = ((bf16[32,2,16384]{2,1,0:T(2,128)(2,1)}), bf16[32,2,16384]{2,1,0:T(2,128)(2,1)S(1)}, u32[]{:S(2)}, u32[]{:S(2)}) async-start(bf16[32,2,16384]{2,1,0:T(2,128)(2,1)} %reshape.133), calls=%async_computation | async-start | bytes 4194304 | tf_op jit(solution)/shard_map/all_to_all | solution.py:30
  102.4 0.0 reduce-scatter.2.cloned.1.call-start
  102.5 0.1 compare_select_fusion
  102.5 0.1 reshape.114
  102.6 0.1 iota_add_fusion
  102.7 0.1 add.104
  102.8 48.5 %all-to-all-done = bf16[32,2,16384]{2,1,0:T(2,128)(2,1)S(1)} async-done(((bf16[32,2,16384]{2,1,0:T(2,128)(2,1)}), bf16[32,2,16384]{2,1,0:T(2,128)(2,1)S(1)}, u32[]{:S(2)}, u32[]{:S(2)}) %all-to-all-start) | async-done | bytes 2097184 | tf_op jit(solution)/shard_map/all_to_all | solution.py:30
  151.3 14.4 %reshape.134 = bf16[4096,16,16]{2,1,0:T(8,128)(2,1)} reshape(bf16[32,2,16384]{2,1,0:T(2,128)(2,1)S(1)} %all-to-all-done) | data formatting | bytes 4194304
  165.7 14.4 %copy.61 = bf16[32,16,16,128]{3,2,1,0:T(8,128)(2,1)S(1)} copy(bf16[32,16,16,128]{2,1,3,0:T(8,128)(2,1)} %bitcast.45) | data formatting | bytes 4194304 | tf_op jit(solution)/shard_map/all_to_all | solution.py:30
  180.1 1.6 gather_fusion
  181.7 1.4 fusion.22
  183.1 60.2 %psum.14 = f32[8]{0:T(128)S(1)} all-reduce(f32[8]{0:T(128)S(1)} %fusion.22), channel_id=1, replica_groups=mesh['tm'=32,'eval'=8] {'tm'}, use_global_device_ids=true, to_apply=%region_3.0 | all-reduce | flops 8 | bytes 64 | tf_op jit(solution)/shard_map/psum | solution.py:37
  243.4 1.3 fusion.23
  244.7 2.3 broadcast_in_dim.2
  247.0 19.7 %scatter_fusion = f32[512,16,128]{2,1,0:T(8,128)} fusion(f32[512,16,128]{2,1,0:T(8,128)} %broadcast_in_dim.2, s32[168]{0:T(256)S(1)} %bitcast.59, f32[168,16,128]{2,1,0:T(8,128)S(1)} %bitcast.50), kind=kCustom, calls=%fused_computation.1 | custom fusion | flops 344064 | bytes 4129440 | tf_op jit(solution)/shard_map/scatter-add | solution.py:44
  266.7 83.4 %all_to_all.36 = f32[512,16,128]{2,1,0:T(8,128)S(1)} all-to-all(f32[512,16,128]{2,1,0:T(8,128)} %scatter_fusion), channel_id=1, replica_groups=mesh['tm'=32,'eval'=8] {'tm'}, dimensions={0} | all-to-all | bytes 8388608 | tf_op jit(solution)/shard_map/all_to_all | solution.py:46
  350.1 2.5 copy.84
  352.7 0.0 reduce-scatter.2.cloned.1.call-update
  352.7 0.0 all-gather.6.cloned.1.call-start
  352.7 50.7 %reduce-scatter.2.cloned.1.call-done = f32[16,16,512]{2,1,0:T(8,128)} async-done(((f32[16,16,4096]{2,1,0:T(8,128)}), f32[16,16,512]{2,1,0:T(8,128)}) %reduce-scatter.2.cloned.1.call-update) | async-done | bytes 524304 | tf_op jit(solution)/shard_map/reduce_scatter | solution.py:47
  403.4 1.1 convert_element_type.43
  404.5 2.0 copy.63
  406.5 2.4 copy.64
  408.8 10.0 %fusion.12 = (f32[16,1536]{1,0:T(8,128)S(1)}, f32[16,128]{1,0:T(8,128)S(1)}, f32[16,128]{1,0:T(8,128)S(1)}, f32[16,1536]{1,0:T(8,128)S(1)}, f32[16,128,1536]{2,1,0:T(8,128)}) fusion(bf16[16,128,1536]{2,1,0:T(8,128)(2,1)} %param.7, f32[16,128]{1,0:T(8,128)S(1)} %add_rsqrt_fusion, f32[16,128]{1,0:T(8,128)S(1)} %broadcast_multiply_fusion.2, ...), kind=kOutput, calls=%fused_computation.16 | convolution fusion | flops 434057216 | bytes 19660800 | tf_op jit(solution)/shard_map/fto,od->ftd/dot_general | solution.py:50
  418.8 0.7 pad_maximum_fusion
  419.5 0.0 all-gather.6.cloned.1.call-update
  419.5 0.0 all-reduce.2.cloned.1.call-start
  419.6 5.6 fusion.18
  425.2 0.0 all-reduce.2.cloned.1.call-update
  425.2 10.5 %fusion.11 = bf16[16,128,1536]{2,1,0:T(8,128)(2,1)} fusion(bf16[16,128,1536]{2,1,0:T(8,128)(2,1)} %param.7, f32[16,128,1536]{2,1,0:T(8,128)} %get-tuple-element.12, f32[16,128]{1,0:T(8,128)S(1)} %broadcast_multiply_fusion, f32[16,128]{1,0:T(8,128)S(1)} %broadcast_multiply_fusion.1, f32[16,1536]{1,0:T(8,128)S(1)} %get-tuple-element.14, ...), kind=kLoop, calls=%fused_computation.15 | loop fusion | flops 28311552 | bytes 25296896 | tf_op jit(solution)/shard_map/convert_element_type | solution.py:61
  435.7 12.9 %all-gather.6.cloned.1.call-done = f32[128,2,1536]{2,0,1:T(8,128)} async-done(((f32[16,2,1536]{2,0,1:T(8,128)}), f32[128,2,1536]{2,0,1:T(8,128)}) %all-gather.6.cloned.1.call-update) | async-done | bytes 1572880 | tf_op jit(solution)/shard_map/all_gather | solution.py:54
  448.6 1.5 reduce_sum.79
  450.1 0.8 copy.67
  451.0 255.0 %all-reduce.2.cloned.1.call-done = f32[64,1536]{1,0:T(8,128)} async-done(((f32[64,1536]{1,0:T(8,128)}), f32[64,1536]{1,0:T(8,128)}) %all-reduce.2.cloned.1.call-update) | async-done | bytes 393232 | tf_op jit(solution)/shard_map/psum | solution.py:53
  705.9 1.8 copy.87
  (18 shorter events, 0.1 us)
Async XLA Ops:
  7.2 8.7 %copy-start = (bf16[64,1536]{1,0:T(8,128)(2,1)S(1)}, bf16[64,1536]{1,0:T(8,128)(2,1)}, u32[]{:S(2)}) copy-start(bf16[64,1536]{1,0:T(8,128)(2,1)} %param.9) | copy-start | bytes 589828
  7.2 8.5 %copy-start.3 = (f32[16,2,1536]{2,1,0:T(2,128)S(1)}, f32[16,2,1536]{2,1,0:T(2,128)}, u32[]{:S(2)}) copy-start(f32[16,2,1536]{2,1,0:T(2,128)} %param.8) | copy-start | bytes 589828
  7.2 49.5 %all-gather.4.cloned.1.call-start = ((), (), s32[]{:S(2)}) async-start(), calls=%async_computation.3 | async-start | bytes 2359296 | tf_op jit(solution)/shard_map/all_gather | solution.py:29
  7.2 8.7 %copy-start.1 = (bf16[16,128,1536]{2,1,0:T(8,128)(2,1)S(1)}, bf16[16,128,1536]{2,1,0:T(8,128)(2,1)}, u32[]{:S(2)}) copy-start(bf16[16,128,1536]{2,1,0:T(8,128)(2,1)} %param.7) | copy-start | bytes 18874372
  72.0 30.4 %copy-start.4 = (s32[8]{0:T(128)S(1)}, s32[8]{0:T(128)}, u32[]{:S(2)}) copy-start(s32[8]{0:T(128)} %param.12) | copy-start | bytes 100
  92.8 58.5 %all-to-all-start = ((bf16[32,2,16384]{2,1,0:T(2,128)(2,1)}), bf16[32,2,16384]{2,1,0:T(2,128)(2,1)S(1)}, u32[]{:S(2)}, u32[]{:S(2)}) async-start(bf16[32,2,16384]{2,1,0:T(2,128)(2,1)} %reshape.133), calls=%async_computation | async-start | bytes 4194304 | tf_op jit(solution)/shard_map/all_to_all | solution.py:30
  102.4 301.0 %reduce-scatter.2.cloned.1.call-start = ((), (), s32[]{:S(2)}) async-start(), calls=%async_computation.4 | async-start | bytes 4718592 | tf_op jit(solution)/shard_map/reduce_scatter | solution.py:47
  165.7 16.0 %copy-start.2 = (bf16[8,21,16,128]{3,2,1,0:T(8,128)(2,1)S(1)}, bf16[8,21,16,128]{3,2,1,0:T(8,128)(2,1)}, u32[]{:S(2)}) copy-start(bf16[8,21,16,128]{3,2,1,0:T(8,128)(2,1)} %param.10) | copy-start | bytes 2064388
  165.7 77.7 %copy-start.5 = (s32[8]{0:T(128)S(1)}, s32[8]{0:T(128)}, u32[]{:S(2)}) copy-start(s32[8]{0:T(128)} %param.13) | copy-start | bytes 100
  352.7 95.9 %all-gather.6.cloned.1.call-start = ((), (), s32[]{:S(2)}) async-start(), calls=%async_computation.6 | async-start | bytes 1769472 | tf_op jit(solution)/shard_map/all_gather | solution.py:54
  419.5 286.4 %all-reduce.2.cloned.1.call-start = ((), (), s32[]{:S(2)}) async-start(), calls=%async_computation.5 | async-start | bytes 786432 | tf_op jit(solution)/shard_map/psum | solution.py:53
Sparse Core Ops, SparseCore 0:
  24.6 31.9 all-gather.3
  352.8 50.5 reduce-scatter.1
  419.6 28.9 all-gather.5
  454.6 251.3 all-reduce.1
